TPU v7x, 128 devices: a whole 4x4x4 slice. The times are simulated.
128 devices in a mesh: expert: 8 (over z, core), fsdp: 16 (over y, x).
Axes of the slice: x: 4, y: 4, z: 4, core: 2. Of those that a mesh axis runs over, the one named last changes fastest.
Arguments:
- tokens: bfloat16 [32768, 2048], P(('expert', 'fsdp')), may hold values from -6 to 6
- expert_ids: int32 [32768, 6], P(('expert', 'fsdp')), may hold values from 0 to 63, as said below
- gate_vals: bfloat16 [32768, 6], P(('expert', 'fsdp')), may hold values from 0.099609375 to 1
- w_gate: bfloat16 [8, 2048, 1408], P('expert', 'fsdp'), may hold values from -0.125 to 0.125
- w_up: bfloat16 [8, 2048, 1408], P('expert', 'fsdp'), may hold values from -0.125 to 0.125
- w_down: bfloat16 [8, 2048, 1408], P('expert', 'fsdp'), may hold values from -0.15625 to 0.15625
- cotangent: bfloat16 [32768, 2048], P(('expert', 'fsdp')), may hold values from -6 to 6
Outputs:
- output: bfloat16 [32768, 2048], P(('expert', 'fsdp'))
- grad_tokens: bfloat16 [32768, 2048], P(('expert', 'fsdp'))
- grad_gates: float32 [32768, 6], P(('expert', 'fsdp'))
- grad_w_gate: float32 [8, 2048, 1408], P('expert', 'fsdp')
- grad_w_up: float32 [8, 2048, 1408], P('expert', 'fsdp')
- grad_w_down: float32 [8, 2048, 1408], P('expert', 'fsdp')
Inputs may be any that keep to these rules, and one draw needn't show every extreme that they name: `expert_ids`: each row names 6 different experts. Among the tokens of one device at most 48 name any one expert whose number modulo 8 is below 1. On every device some such expert is named by exactly 48 of its tokens, and for every column one such expert is named by exactly 48 tokens of every device of that column.
All inputs are finite; a program needn't handle non-finite values.
Results may differ from a plain program's by a relative error of at most 0.013.
Values may be sent and summed in bfloat16 or wider, within the bound.
No kernel may reach another device: no remote copies, remote signals or barrier semaphores. Data moves between devices by JAX's collectives and lax.ppermute only.
A program may use at most 128 MiB of HBM per device.

v0:
```python
import jax
import jax.numpy as jnp
from jax import lax
from jax.sharding import PartitionSpec as P

EXPERTS = 64
TOP = 6
WAVE = 1
MOST = 48


def slot_tables(expert_ids, groups):
    per_index = EXPERTS // groups
    window = WAVE * groups
    tok_count = expert_ids.shape[0]
    flat_ids = expert_ids.reshape(-1)
    local_index = flat_ids % per_index
    is_live = local_index < WAVE
    window_slot = jnp.where(is_live, flat_ids // per_index * WAVE + local_index, window)
    onehot = (window_slot[:, None] == jnp.arange(window, dtype=jnp.int32)[None, :]).astype(
        jnp.int32
    )
    rank_in = jnp.sum((jnp.cumsum(onehot, axis=0) - 1) * onehot, axis=1)
    target = jnp.where(is_live, window_slot * MOST + rank_in, window * MOST)
    slot_ids = jnp.arange(tok_count * TOP, dtype=jnp.int32)
    source = (
        jnp.full((window * MOST,), tok_count * TOP, jnp.int32).at[target].set(slot_ids, mode="drop")
    )
    return (target, source)


def on_device(tokens, expert_ids, gate_vals, w_gate, w_up, w_down, cotangent):
    groups = lax.axis_size("expert")
    tok_count, model_width = tokens.shape
    target, source = slot_tables(expert_ids, groups)
    token_of = source // TOP
    zero_row = jnp.zeros((1, model_width), jnp.bfloat16)
    tokens_pad = jnp.concatenate([tokens, zero_row], axis=0)
    cot_pad = jnp.concatenate([cotangent, zero_row], axis=0)
    gate_pad = jnp.concatenate([gate_vals.reshape(-1), jnp.zeros((1,), jnp.bfloat16)], axis=0)
    send_rows = tokens_pad[token_of].reshape(groups, WAVE * MOST, model_width)
    arrived = lax.all_to_all(send_rows, "expert", split_axis=0, concat_axis=0, tiled=True)
    rows_in = arrived.reshape(groups, WAVE, MOST, model_width)
    full_gate, full_up, full_down = (
        lax.all_gather(w_gate, "fsdp", axis=1, tiled=True),
        lax.all_gather(w_up, "fsdp", axis=1, tiled=True),
        lax.all_gather(w_down, "fsdp", axis=1, tiled=True),
    )
    gate_pre = jnp.einsum("skmd,kdf->skmf", rows_in, full_gate, preferred_element_type=jnp.float32)
    up_pre = jnp.einsum("skmd,kdf->skmf", rows_in, full_up, preferred_element_type=jnp.float32)
    sigmoid_g = jax.nn.sigmoid(gate_pre)
    hidden = (gate_pre * sigmoid_g * up_pre).astype(jnp.bfloat16)
    expert_out = jnp.einsum(
        "skmf,kdf->skmd", hidden, full_down, preferred_element_type=jnp.float32
    ).astype(jnp.bfloat16)
    returned = lax.all_to_all(
        expert_out.reshape(groups, WAVE * MOST, model_width),
        "expert",
        split_axis=0,
        concat_axis=0,
        tiled=True,
    )
    back_pad = jnp.concatenate([returned.reshape(-1, model_width), zero_row], axis=0)
    slot_out = back_pad[target].reshape(tok_count, TOP, model_width).astype(jnp.float32)
    output = jnp.sum(gate_vals.astype(jnp.float32)[:, :, None] * slot_out, axis=1).astype(
        jnp.bfloat16
    )
    grad_gates = jnp.sum(cotangent.astype(jnp.float32)[:, None, :] * slot_out, axis=2)
    gate_rows = gate_pad[source].astype(jnp.float32)
    send_grad = (gate_rows[:, None] * cot_pad[token_of].astype(jnp.float32)).astype(jnp.bfloat16)
    grad_in = lax.all_to_all(
        send_grad.reshape(groups, WAVE * MOST, model_width),
        "expert",
        split_axis=0,
        concat_axis=0,
        tiled=True,
    )
    out_grad = grad_in.reshape(groups, WAVE, MOST, model_width)
    hidden_grad = jnp.einsum(
        "skmd,kdf->skmf", out_grad, full_down, preferred_element_type=jnp.float32
    )
    gate_grad = (hidden_grad * up_pre * sigmoid_g * (1.0 + gate_pre * (1.0 - sigmoid_g))).astype(
        jnp.bfloat16
    )
    up_grad = (hidden_grad * gate_pre * sigmoid_g).astype(jnp.bfloat16)
    row_grad = (
        jnp.einsum("skmf,kdf->skmd", gate_grad, full_gate, preferred_element_type=jnp.float32)
        + jnp.einsum("skmf,kdf->skmd", up_grad, full_up, preferred_element_type=jnp.float32)
    ).astype(jnp.bfloat16)
    grads_home = lax.all_to_all(
        row_grad.reshape(groups, WAVE * MOST, model_width),
        "expert",
        split_axis=0,
        concat_axis=0,
        tiled=True,
    )
    grads_pad = jnp.concatenate([grads_home.reshape(-1, model_width), zero_row], axis=0)
    grad_tokens = jnp.sum(
        grads_pad[target].reshape(tok_count, TOP, model_width).astype(jnp.float32), axis=1
    ).astype(jnp.bfloat16)
    term_gate = jnp.einsum("skmd,skmf->kdf", rows_in, gate_grad, preferred_element_type=jnp.float32)
    term_up = jnp.einsum("skmd,skmf->kdf", rows_in, up_grad, preferred_element_type=jnp.float32)
    term_down = jnp.einsum("skmd,skmf->kdf", out_grad, hidden, preferred_element_type=jnp.float32)
    grad_w_gate, grad_w_up, grad_w_down = (
        lax.psum_scatter(
            term_gate.astype(jnp.bfloat16), "fsdp", scatter_dimension=1, tiled=True
        ).astype(jnp.float32),
        lax.psum_scatter(
            term_up.astype(jnp.bfloat16), "fsdp", scatter_dimension=1, tiled=True
        ).astype(jnp.float32),
        lax.psum_scatter(
            term_down.astype(jnp.bfloat16), "fsdp", scatter_dimension=1, tiled=True
        ).astype(jnp.float32),
    )
    return (output, grad_tokens, grad_gates, grad_w_gate, grad_w_up, grad_w_down)


def solution(mesh):
    placed = (
        P(("expert", "fsdp"), None),
        P(("expert", "fsdp"), None),
        P(("expert", "fsdp"), None),
        P("expert", "fsdp", None),
        P("expert", "fsdp", None),
        P("expert", "fsdp", None),
        P(("expert", "fsdp"), None),
    )
    return jax.shard_map(
        on_device,
        mesh=mesh,
        in_specs=placed,
        out_specs=(
            P(("expert", "fsdp"), None),
            P(("expert", "fsdp"), None),
            P(("expert", "fsdp"), None),
            P("expert", "fsdp", None),
            P("expert", "fsdp", None),
            P("expert", "fsdp", None),
        ),
        check_vma=False,
    )
```

profile of v0, /device:TPU:0, one launch (start us, length us, event | category | flops | bytes accessed | tf_op | source)
XLA Modules:
  0.0 461.0 jit_solution(18036882781366785138)
XLA Ops:
  7.2 0.7 all-gather.8.cloned.1.call-update
  8.0 0.7 all-gather.6.cloned.1.call-update
  9.4 0.8 copy.20
  10.7 0.8 copy.23
  11.7 2.3 reduce-window.6
  14.7 6.2 %scatter_custom_fusion = s32[384]{0:T(512)S(1)} fusion(s32[1536]{0:T(1024)S(1)} %get-tuple-element.15, s32[1536]{0:T(1024)S(1)} %iota.11, s32[]{:T(128)} %constant.52.clone.1), kind=kCustom, calls=%fused_computation.94 | custom fusion | bytes 1540 | tf_op jit(solution)/shard_map/scatter | solution.py:27
  20.9 2.8 gather_fusion.2
  23.9 2.5 gather_fusion.3
  26.4 1.5 fusion.15
  27.9 5.4 %all-to-all-start.2 = ((bf16[8,48,2048]{2,1,0:T(8,128)(2,1)}), bf16[8,48,2048]{2,1,0:T(8,128)(2,1)S(1)}, u32[]{:S(2)}, u32[]{:S(2)}) async-start(bf16[8,48,2048]{2,1,0:T(8,128)(2,1)} %fusion.15), calls=%async_computation.2 | async-start | bytes 3145728 | tf_op jit(solution)/shard_map/all_to_all | solution.py:71
  33.3 1.3 concatenate.15
  34.6 3.1 gather_fusion
  37.7 17.1 %all-to-all-done.2 = bf16[8,48,2048]{2,1,0:T(8,128)(2,1)S(1)} async-done(((bf16[8,48,2048]{2,1,0:T(8,128)(2,1)}), bf16[8,48,2048]{2,1,0:T(8,128)(2,1)S(1)}, u32[]{:S(2)}, u32[]{:S(2)}) %all-to-all-start.2) | async-done | bytes 1572896 | tf_op jit(solution)/shard_map/all_to_all | solution.py:71
  54.9 3.6 all-to-all-start
  58.5 12.8 %all-gather.8.cloned.1.call-done = bf16[1,2048,1408]{2,1,0:T(8,128)(2,1)} async-done(((bf16[1,128,1408]{2,1,0:T(8,128)(2,1)}), bf16[1,2048,1408]{2,1,0:T(8,128)(2,1)}) %all-gather.8.cloned.1.call-update) | async-done | bytes 5767184 | tf_op jit(solution)/shard_map/all_gather | solution.py:47
  71.4 6.6 %fusion.22 = f32[8,1,48,1408]{3,2,0,1:T(8,128)} fusion(bf16[8,48,2048]{2,1,0:T(8,128)(2,1)S(1)} %all-to-all-done.2, bf16[1,2048,1408]{2,1,0:T(8,128)(2,1)} %all-gather.8.cloned.1.call-done), kind=kOutput, calls=%fused_computation.31 | convolution fusion | flops 2214592512 | bytes 9502720 | tf_op jit(solution)/shard_map/skmd,kdf->skmf/dot_general | solution.py:79
  78.0 2.0 all-to-all-done
  80.0 52.0 %all-gather.6.cloned.1.call-done = bf16[1,2048,1408]{2,1,0:T(8,128)(2,1)} async-done(((bf16[1,128,1408]{2,1,0:T(8,128)(2,1)}), bf16[1,2048,1408]{2,1,0:T(8,128)(2,1)}) %all-gather.6.cloned.1.call-update) | async-done | bytes 5767184 | tf_op jit(solution)/shard_map/all_gather | solution.py:46
  132.0 6.6 %fusion.19 = f32[8,1,48,1408]{3,2,0,1:T(8,128)} fusion(bf16[8,48,2048]{2,1,0:T(8,128)(2,1)S(1)} %all-to-all-done, bf16[1,2048,1408]{2,1,0:T(8,128)(2,1)} %all-gather.6.cloned.1.call-done), kind=kOutput, calls=%fused_computation.30 | convolution fusion | flops 2214592512 | bytes 9502720 | tf_op jit(solution)/shard_map/skmd,kdf->skmf/dot_general | solution.py:50
  138.6 54.0 %all-gather.4.cloned.1.call-done = bf16[1,2048,1408]{2,1,0:T(8,128)(2,1)} async-done(((bf16[1,128,1408]{2,1,0:T(8,128)(2,1)}), bf16[1,2048,1408]{2,1,0:T(8,128)(2,1)}) %all-gather.4.cloned.1.call-update) | async-done | bytes 5767184 | tf_op jit(solution)/shard_map/all_gather | solution.py:45
  192.6 7.9 %multiply_convert_fusion.1 = (bf16[8,1,48,1408]{3,2,0,1:T(8,128)(2,1)}, bf16[8,1,48,1408]{3,2,0,1:T(8,128)(2,1)S(1)}, bf16[8,1,48,1408]{3,2,0,1:T(8,128)(2,1)}) fusion(f32[8,1,48,1408]{3,2,0,1:T(8,128)} %fusion.22, f32[8,1,48,1408]{3,2,0,1:T(8,128)} %fusion.19, bf16[8,48,2048]{2,1,0:T(8,128)(2,1)S(1)} %all-to-all-done, ...), kind=kOutput, calls=%fused_computation.34 | convolution fusion | flops 2223243264 | bytes 14909440 | tf_op jit(solution)/shard_map/skmd,kdf->skmf/dot_general | solution.py:49
  200.5 1.0 copy-done.5
  201.5 5.2 %fusion.2 = bf16[1,2048,1408]{2,1,0:T(8,128)(2,1)} fusion(bf16[8,48,2048]{2,1,0:T(8,128)(2,1)S(1)} %all-to-all-done.2, bf16[8,1,48,1408]{3,2,0,1:T(8,128)(2,1)S(1)} %get-tuple-element.17), kind=kOutput, calls=%fused_computation.13 | convolution fusion | flops 2217476096 | bytes 8421376 | tf_op jit(solution)/shard_map/skmd,skmf->kdf/dot_general | solution.py:103
  206.9 1.0 copy-done.7
  207.9 5.1 %fusion = bf16[1,2048,1408]{2,1,0:T(8,128)(2,1)} fusion(bf16[8,48,2048]{2,1,0:T(8,128)(2,1)S(1)} %all-to-all-done, bf16[8,1,48,1408]{3,2,0,1:T(8,128)(2,1)S(1)} %copy-done.7), kind=kOutput, calls=%fused_computation.11 | convolution fusion | flops 2217476096 | bytes 8421376 | tf_op jit(solution)/shard_map/skmd,skmf->kdf/dot_general | solution.py:101
  213.1 1.2 copy-done.4
  214.3 5.1 %fusion.1 = bf16[1,2048,1408]{2,1,0:T(8,128)(2,1)} fusion(bf16[8,48,2048]{2,1,0:T(8,128)(2,1)S(1)} %all-to-all-done, bf16[8,1,48,1408]{3,2,0,1:T(8,128)(2,1)S(1)} %copy-done.4), kind=kOutput, calls=%fused_computation.12 | convolution fusion | flops 2217476096 | bytes 8421376 | tf_op jit(solution)/shard_map/skmd,skmf->kdf/dot_general | solution.py:102
  219.4 1.2 copy-done.6
  220.6 7.8 %fusion.27 = bf16[8,48,2048]{2,1,0:T(8,128)(2,1)} fusion(bf16[1,2048,1408]{2,1,0:T(8,128)(2,1)} %all-gather.8.cloned.1.call-done, bf16[8,1,48,1408]{3,2,0,1:T(8,128)(2,1)S(1)} %copy-done.6), kind=kOutput, calls=%fused_computation.32 | convolution fusion | flops 2215378944 | bytes 8421376 | tf_op jit(solution)/shard_map/skmf,kdf->skmd/dot_general | solution.py:53
  228.4 4.6 all-to-all-start.1
  232.9 5.2 %fusion.7 = f32[8,48,2048]{2,1,0:T(8,128)S(1)} fusion(bf16[1,2048,1408]{2,1,0:T(8,128)(2,1)} %all-gather.6.cloned.1.call-done, bf16[8,1,48,1408]{3,2,0,1:T(8,128)(2,1)} %get-tuple-element.18), kind=kOutput, calls=%fused_computation.18 | convolution fusion | flops 2214592512 | bytes 9994240 | tf_op jit(solution)/shard_map/skmf,kdf->skmd/dot_general | solution.py:88
  238.2 3.8 add_convert_fusion
  242.0 12.5 %all-to-all-done.1 = bf16[8,48,2048]{2,1,0:T(8,128)(2,1)S(1)} async-done(((bf16[8,48,2048]{2,1,0:T(8,128)(2,1)}), bf16[8,48,2048]{2,1,0:T(8,128)(2,1)S(1)}, u32[]{:S(2)}, u32[]{:S(2)}) %all-to-all-start.1) | async-done | bytes 1572896 | tf_op jit(solution)/shard_map/all_to_all | solution.py:56
  254.5 4.3 all-to-all-start.3
  259.0 1.6 convert_element_type.110
  260.8 19.6 %all-to-all-done.3 = bf16[8,48,2048]{2,1,0:T(8,128)(2,1)} async-done(((bf16[8,48,2048]{2,1,0:T(8,128)(2,1)}), bf16[8,48,2048]{2,1,0:T(8,128)(2,1)}, u32[]{:S(2)}, u32[]{:S(2)}) %all-to-all-start.3) | async-done | bytes 1572896 | tf_op jit(solution)/shard_map/all_to_all | solution.py:90
  280.4 1.5 concatenate.19
  281.9 7.1 %gather_fusion.4 = bf16[1536,2048]{1,0:T(8,128)(2,1)} fusion(bf16[385,2048]{1,0:T(8,128)(2,1)S(1)} %concatenate.19, s32[2048]{0:T(1024)S(1)} %pad_clamp_fusion), kind=kCustom, calls=%fused_computation.4 | custom fusion | bytes 12589056 | tf_op jit(solution)/shard_map/gather | solution.py:99
  289.0 11.0 %reshape.325 = bf16[256,6,2048]{2,1,0:T(8,128)(2,1)} reshape(bf16[1536,2048]{1,0:T(8,128)(2,1)} %gather_fusion.4) | data formatting | bytes 12582912 | tf_op jit(solution)/shard_map/reshape | solution.py:99
  300.0 9.7 %reduce_sum.44 = bf16[256,2048]{1,0:T(8,128)(2,1)} reduce(bf16[256,6,2048]{2,1,0:T(8,128)(2,1)} %reshape.325, bf16[]{:T(256)} %constant.31.clone.1), dimensions={1}, to_apply=%region_5.6 | reduce | flops 2621440 | bytes 7340034 | tf_op jit(solution)/shard_map/reduce_sum | solution.py:98
  309.8 7.1 %gather_fusion.1 = bf16[1536,2048]{1,0:T(8,128)(2,1)} fusion(bf16[385,2048]{1,0:T(8,128)(2,1)S(1)} %concatenate.16, s32[2048]{0:T(1024)S(1)} %pad_clamp_fusion), kind=kCustom, calls=%fused_computation.1 | custom fusion | bytes 12589056 | tf_op jit(solution)/shard_map/gather | solution.py:64
  316.9 12.0 %reshape.326 = f32[256,6,2048]{2,1,0:T(8,128)} reshape(bf16[1536,2048]{1,0:T(8,128)(2,1)} %gather_fusion.1) | data formatting | bytes 18874368 | tf_op jit(solution)/shard_map/convert_element_type | solution.py:64
  328.9 11.9 %multiply_reduce_fusion = (f32[256,6]{1,0:T(8,128)S(1)}, bf16[256,2048]{1,0:T(8,128)(2,1)}) fusion(f32[256,6,2048]{2,1,0:T(8,128)} %reshape.326, f32[256,2048]{1,0:T(8,128)S(1)} %copy-done, f32[256,6]{1,0:T(8,128)S(1)} %copy.19), kind=kLoop, calls=%fused_computation.6 | loop fusion | flops 12057088 | bytes 15740928 | tf_op jit(solution)/shard_map/reduce_sum | solution.py:68
  341.5 1.9 convert_element_type.119
  343.4 26.1 %reduce-scatter.4.cloned.1.call-done = bf16[1,128,1408]{2,1,0:T(8,128)(2,1)} async-done(((bf16[1,2048,1408]{2,1,0:T(8,128)(2,1)}), bf16[1,128,1408]{2,1,0:T(8,128)(2,1)}) %reduce-scatter.4.cloned.1.call-update) | async-done | bytes 360464 | tf_op jit(solution)/shard_map/reduce_scatter | solution.py:105
  369.5 1.9 convert_element_type.113
  371.4 80.9 %reduce-scatter.6.cloned.1.call-done = bf16[1,128,1408]{2,1,0:T(8,128)(2,1)} async-done(((bf16[1,2048,1408]{2,1,0:T(8,128)(2,1)}), bf16[1,128,1408]{2,1,0:T(8,128)(2,1)}) %reduce-scatter.6.cloned.1.call-update) | async-done | bytes 360464 | tf_op jit(solution)/shard_map/reduce_scatter | solution.py:108
  452.3 1.9 convert_element_type.116
  (52 shorter events, 3.7 us)
Async XLA Ops:
  7.2 16.6 %copy-start.1 = (bf16[256,2048]{1,0:T(8,128)(2,1)S(1)}, bf16[256,2048]{1,0:T(8,128)(2,1)}, u32[]{:S(2)}) copy-start(bf16[256,2048]{1,0:T(8,128)(2,1)} %param.13) | copy-start | bytes 3145732
  7.2 64.2 %all-gather.8.cloned.1.call-start = ((), (), s32[]{:S(2)}) async-start(), calls=%async_computation.9 | async-start | bytes 6127616 | tf_op jit(solution)/shard_map/all_gather | solution.py:47
  7.9 124.1 %all-gather.6.cloned.1.call-start = ((), (), s32[]{:S(2)}) async-start(), calls=%async_computation.8 | async-start | bytes 6127616 | tf_op jit(solution)/shard_map/all_gather | solution.py:46
  8.7 184.0 %all-gather.4.cloned.1.call-start = ((), (), s32[]{:S(2)}) async-start(), calls=%async_computation.7 | async-start | bytes 6127616 | tf_op jit(solution)/shard_map/all_gather | solution.py:45
  27.9 27.0 %all-to-all-start.2 = ((bf16[8,48,2048]{2,1,0:T(8,128)(2,1)}), bf16[8,48,2048]{2,1,0:T(8,128)(2,1)S(1)}, u32[]{:S(2)}, u32[]{:S(2)}) async-start(bf16[8,48,2048]{2,1,0:T(8,128)(2,1)} %fusion.15), calls=%async_computation.2 | async-start | bytes 3145728 | tf_op jit(solution)/shard_map/all_to_all | solution.py:71
  54.9 25.1 %all-to-all-start = ((bf16[8,48,2048]{2,1,0:T(8,128)(2,1)}), bf16[8,48,2048]{2,1,0:T(8,128)(2,1)S(1)}, u32[]{:S(2)}, u32[]{:S(2)}) async-start(bf16[8,48,2048]{2,1,0:T(8,128)(2,1)} %bitcast.1), calls=%async_computation | async-start | bytes 3145728 | tf_op jit(solution)/shard_map/all_to_all | solution.py:42
  58.5 283.0 %reduce-scatter.8.cloned.1.call-start = ((), (), s32[]{:S(2)}) async-start(), calls=%async_computation.12 | async-start | bytes 6127616 | tf_op jit(solution)/shard_map/reduce_scatter | solution.py:111
  200.5 1.0 copy-start.5
  206.7 1.2 copy-start.7
  206.7 162.8 %reduce-scatter.4.cloned.1.call-start = ((), (), s32[]{:S(2)}) async-start(), calls=%async_computation.10 | async-start | bytes 6127616 | tf_op jit(solution)/shard_map/reduce_scatter | solution.py:105
  213.0 1.2 copy-start.4
  213.1 239.2 %reduce-scatter.6.cloned.1.call-start = ((), (), s32[]{:S(2)}) async-start(), calls=%async_computation.11 | async-start | bytes 6127616 | tf_op jit(solution)/shard_map/reduce_scatter | solution.py:108
  219.4 1.2 copy-start.6
  228.4 9.8 %slice-start = ((s8[5767168]{0:T(1024)(128)(4,1)}), s8[1572864]{0:T(1024)(128)(4,1)S(1)}, s32[]{:S(2)}) async-start(s8[5767168]{0:T(1024)(128)(4,1)} %bitcast.111), calls=%async_computation.13 | async-start | bytes 3145728
  228.4 26.1 %all-to-all-start.1 = ((bf16[8,48,2048]{2,1,0:T(8,128)(2,1)}), bf16[8,48,2048]{2,1,0:T(8,128)(2,1)S(1)}, u32[]{:S(2)}, u32[]{:S(2)}) async-start(bf16[8,48,2048]{2,1,0:T(8,128)(2,1)} %fusion.27), calls=%async_computation.1 | async-start | bytes 3145728 | tf_op jit(solution)/shard_map/all_to_all | solution.py:56
  232.9 5.2 %slice-start.1 = ((s8[5767168]{0:T(1024)(128)(4,1)}), s8[4194304]{0:T(1024)(128)(4,1)S(1)}, s32[]{:S(2)}) async-start(s8[5767168]{0:T(1024)(128)(4,1)} %bitcast.111), calls=%async_computation.14 | async-start | bytes 8388608
  232.9 5.2 %copy-start.8 = (bf16[8,1,48,1408]{3,2,0,1:T(8,128)(2,1)S(1)}, bf16[8,1,48,1408]{3,2,0,1:T(8,128)(2,1)}, u32[]{:S(2)}) copy-start(bf16[8,1,48,1408]{3,2,0,1:T(8,128)(2,1)} %get-tuple-element.16) | copy-start | bytes 3244036
  242.0 16.8 %copy-start.3 = (bf16[256,6]{0,1:T(8,128)(2,1)S(1)}, bf16[256,6]{0,1:T(8,128)(2,1)}, u32[]{:S(2)}) copy-start(bf16[256,6]{0,1:T(8,128)(2,1)} %param.9) | copy-start | bytes 9220
  242.0 16.9 %copy-start.2 = (bf16[256,2048]{1,0:T(8,128)(2,1)S(1)}, bf16[256,2048]{1,0:T(8,128)(2,1)}, u32[]{:S(2)}) copy-start(bf16[256,2048]{1,0:T(8,128)(2,1)} %param.13) | copy-start | bytes 3145732
  254.5 25.9 %all-to-all-start.3 = ((bf16[8,48,2048]{2,1,0:T(8,128)(2,1)}), bf16[8,48,2048]{2,1,0:T(8,128)(2,1)}, u32[]{:S(2)}, u32[]{:S(2)}) async-start(bf16[8,48,2048]{2,1,0:T(8,128)(2,1)} %add_convert_fusion), calls=%async_computation.3 | async-start | bytes 3145728 | tf_op jit(solution)/shard_map/all_to_all | solution.py:90
  316.9 12.0 %copy-start = (f32[256,2048]{1,0:T(8,128)S(1)}, f32[256,2048]{1,0:T(8,128)}, u32[]{:S(2)}) copy-start(f32[256,2048]{1,0:T(8,128)} %convert_element_type.110) | copy-start | bytes 6291460
Sparse Core Ops, SparseCore 0:
  10.1 61.1 all-gather.7
  73.5 58.4 all-gather.5
  134.1 58.4 all-gather.3
  206.8 79.7 reduce-scatter.7
  289.8 79.5 reduce-scatter.3
  372.7 79.5 reduce-scatter.5
where the time goes:
time: 463 us; the launch traced here: 461 us
  waiting for transfers between devices  279 us (60%)
  local copies, waits for them, and re-layouts  62.6 us (14%)
  matrix products  53.3 us (12%)
  other arithmetic  33.2 us (7%)
  starting transfers between devices  18.3 us (4%)
  between operations  14.4 us (3%)
    reduce_scatter x1, waiting for transfers between devices, on_device(): lax.psum_scatter(term_up.astype(jnp.bfloat16), 'fsdp', scatter_dimension=...  80.9 us
    all_gather x1, waiting for transfers between devices, on_device(): lax.all_gather(w_gate, 'fsdp', axis=1, tiled=True)  54 us
    all_gather x1, waiting for transfers between devices, on_device(): lax.all_gather(w_up, 'fsdp', axis=1, tiled=True)  52 us
    reduce_scatter x1, waiting for transfers between devices, on_device(): lax.psum_scatter(term_gate.astype(jnp.bfloat16), 'fsdp', scatter_dimensio...  26.1 us
    all_to_all x1, waiting for transfers between devices, on_device(): lax.all_to_all(row_grad.reshape(groups, WAVE * MOST, model_width), 'exper...  19.6 us
    all_to_all x1, waiting for transfers between devices, on_device(): lax.all_to_all(send_grad.reshape(groups, WAVE * MOST, model_width), 'expe...  17.1 us
    all_gather x1, waiting for transfers between devices, on_device(): lax.all_gather(w_down, 'fsdp', axis=1, tiled=True)  12.8 us
    all_to_all x1, waiting for transfers between devices, on_device(): lax.all_to_all(expert_out.reshape(groups, WAVE * MOST, model_width), 'exp...  12.5 us
  transfers between devices with their start and end apart: 10, of which 9 were waited for; matrix products, arithmetic and copies ran while one was open for 28% of the time, Pallas kernels for 0%

commit v1 on v0

--- a/solution.py
+++ b/solution.py
@@ -44,7 +44,9 @@
     full_gate, full_up, full_down = (
         lax.all_gather(w_gate, "fsdp", axis=1, tiled=True),
         lax.all_gather(w_up, "fsdp", axis=1, tiled=True),
-        lax.all_gather(w_down, "fsdp", axis=1, tiled=True),
+        jnp.concatenate(
+            lax.all_to_all(jnp.stack([w_down] * lax.axis_size("fsdp")), "fsdp", 0, 0), axis=1
+        ),
     )
     gate_pre = jnp.einsum("skmd,kdf->skmf", rows_in, full_gate, preferred_element_type=jnp.float32)
     up_pre = jnp.einsum("skmd,kdf->skmf", rows_in, full_up, preferred_element_type=jnp.float32)

time: 463 us -> 460 us (level)
  waiting for transfers between devices: 279 us -> 246 us
  blocking collectives: 0 us -> 27.1 us
    all_to_all x1, waiting for transfers between devices: 17.1 us -> 90 us  [on_device(): lax.all_to_all(jnp.stack([w_down] * lax.axis_size('fsdp')), 'fsdp', 0, 0)]
    all_gather x1, waiting for transfers between devices: 54 us -> 0.34 us  [on_device(): lax.all_gather(w_gate, 'fsdp', axis=1, tiled=True)]
    all_gather x1, waiting for transfers between devices: 52 us -> 0.01 us  [on_device(): lax.all_gather(w_up, 'fsdp', axis=1, tiled=True)]
    all_to_all x0 -> x1, blocking collectives: none -> 27.1 us  [on_device(): lax.all_to_all(send_grad.reshape(groups, WAVE * MOST, model_width), 'expe...]
    reduce_scatter x1, waiting for transfers between devices: 26.1 us -> 45 us  [on_device(): lax.psum_scatter(term_gate.astype(jnp.bfloat16), 'fsdp', scatter_dimensio...]
    all_gather x1 -> x0, waiting for transfers between devices: 12.8 us -> none  [on_device(): lax.all_gather(w_down, 'fsdp', axis=1, tiled=True)]
    all_to_all x1, waiting for transfers between devices: 12.5 us -> 0.01 us  [on_device(): lax.all_to_all(expert_out.reshape(groups, WAVE * MOST, model_width), 'exp...]
    all_to_all x1, waiting for transfers between devices: 1.99 us -> 14.3 us  [on_device(): lax.all_to_all(send_rows, 'expert', split_axis=0, concat_axis=0, tiled=True)]
  transfers between devices with their start and end apart: 10 -> 9, of which waited for: 9 -> 6; matrix products, arithmetic and copies ran while one was open for 28% -> 29% of each run, Pallas kernels for 0% -> 0%
where the time goes in v1:
time: 460 us; the launch traced here: 459 us
  waiting for transfers between devices  246 us (53%)
  local copies, waits for them, and re-layouts  64.7 us (14%)
  matrix products  53.5 us (12%)
  other arithmetic  33.3 us (7%)
  blocking collectives  27.1 us (6%)
  starting transfers between devices  20.6 us (4%)
  between operations  14.1 us (3%)
    all_to_all x1, waiting for transfers between devices, on_device(): lax.all_to_all(jnp.stack([w_down] * lax.axis_size('fsdp')), 'fsdp', 0, 0)  90 us
    reduce_scatter x1, waiting for transfers between devices, on_device(): lax.psum_scatter(term_up.astype(jnp.bfloat16), 'fsdp', scatter_dimension=...  80.7 us
    reduce_scatter x1, waiting for transfers between devices, on_device(): lax.psum_scatter(term_gate.astype(jnp.bfloat16), 'fsdp', scatter_dimensio...  45 us
    all_to_all x1, blocking collectives, on_device(): lax.all_to_all(send_grad.reshape(groups, WAVE * MOST, model_width), 'expe...  27.1 us
    all_to_all x1, waiting for transfers between devices, on_device(): lax.all_to_all(send_rows, 'expert', split_axis=0, concat_axis=0, tiled=True)  14.3 us
    all_to_all x1, waiting for transfers between devices, on_device(): lax.all_to_all(row_grad.reshape(groups, WAVE * MOST, model_width), 'exper...  13.8 us
    convert_element_type x1, local copies, waits for them, and re-layouts, on_device(): back_pad[target].reshape(tok_count, TOP, model_width).astype(jnp.float32)  12 us
    reduce_sum x1, other arithmetic, on_device(): jnp.sum(cotangent.astype(jnp.float32)[:, None, :] * slot_out, axis=2)  11.9 us
  transfers between devices with their start and end apart: 9, of which 6 were waited for; matrix products, arithmetic and copies ran while one was open for 29% of the time, Pallas kernels for 0%

profile of v1, /device:TPU:0, one launch (start us, length us, event | category | flops | bytes accessed | tf_op | source)
XLA Modules:
  0.0 458.8 jit_solution(13977984579217965506)
XLA Ops:
  7.2 0.7 all-gather.5.cloned.1.call-update
  8.0 0.7 all-gather.3.cloned.1.call-update
  8.7 0.8 copy.20
  10.0 2.3 reduce-window.6
  12.2 0.3 slice_reduce_fusion
  12.7 0.8 copy.23
  13.9 6.2 %scatter_custom_fusion = s32[384]{0:T(512)S(1)} fusion(s32[1536]{0:T(1024)S(1)} %get-tuple-element.15, s32[1536]{0:T(1024)S(1)} %iota.11, s32[]{:T(128)} %constant.52.clone.1), kind=kCustom, calls=%fused_computation.90 | custom fusion | bytes 1540 | tf_op jit(solution)/shard_map/scatter | solution.py:27
  20.2 2.8 gather_fusion.2
  23.2 2.5 gather_fusion.3
  25.6 0.3 fusion.11
  26.0 27.1 %all_to_all.25 = bf16[8,48,2048]{2,1,0:T(8,128)(2,1)S(1)} all-to-all(bf16[8,48,2048]{2,1,0:T(8,128)(2,1)S(1)} %fusion.11), channel_id=1, replica_groups=mesh['expert'=8,'fsdp'=16] {'expert'}, dimensions={0} | all-to-all | bytes 3145728 | tf_op jit(solution)/shard_map/all_to_all | solution.py:73
  53.1 3.1 stack.2
  56.2 7.1 %all-to-all-start.1 = ((bf16[16,1,128,1408]{3,2,1,0:T(8,128)(2,1)}), bf16[16,1,128,1408]{3,2,1,0:T(8,128)(2,1)}, u32[]{:S(2)}, u32[]{:S(2)}) async-start(bf16[16,1,128,1408]{3,2,1,0:T(8,128)(2,1)} %stack.2), calls=%async_computation.1 | async-start | bytes 11534336 | tf_op jit(solution)/shard_map/all_to_all | solution.py:48
  63.3 1.3 concatenate.15
  64.6 3.1 gather_fusion
  67.7 90.0 %all-to-all-done.1 = bf16[16,1,128,1408]{3,2,1,0:T(8,128)(2,1)} async-done(((bf16[16,1,128,1408]{3,2,1,0:T(8,128)(2,1)}), bf16[16,1,128,1408]{3,2,1,0:T(8,128)(2,1)}, u32[]{:S(2)}, u32[]{:S(2)}) %all-to-all-start.1) | async-done | bytes 5767200 | tf_op jit(solution)/shard_map/all_to_all | solution.py:48
  157.8 5.0 %all-to-all-start = ((bf16[8,48,2048]{2,1,0:T(8,128)(2,1)}), bf16[8,48,2048]{2,1,0:T(8,128)(2,1)S(1)}, u32[]{:S(2)}, u32[]{:S(2)}) async-start(bf16[8,48,2048]{2,1,0:T(8,128)(2,1)} %bitcast.1), calls=%async_computation | async-start | bytes 3145728 | tf_op jit(solution)/shard_map/all_to_all | solution.py:42
  163.0 7.1 %convolution_bitcast_fusion = f32[8,1,48,1408]{3,2,0,1:T(8,128)} fusion(bf16[8,48,2048]{2,1,0:T(8,128)(2,1)S(1)} %all_to_all.25, bf16[2048,1408,1]{1,0,2:T(8,128)(2,1)} %bitcast.17), kind=kOutput, calls=%fused_computation.27 | convolution fusion | flops 2214592512 | bytes 9502720 | tf_op jit(solution)/shard_map/skmd,kdf->skmf/dot_general | solution.py:81
  170.1 14.3 %all-to-all-done = bf16[8,48,2048]{2,1,0:T(8,128)(2,1)S(1)} async-done(((bf16[8,48,2048]{2,1,0:T(8,128)(2,1)}), bf16[8,48,2048]{2,1,0:T(8,128)(2,1)S(1)}, u32[]{:S(2)}, u32[]{:S(2)}) %all-to-all-start) | async-done | bytes 1572896 | tf_op jit(solution)/shard_map/all_to_all | solution.py:42
  184.3 6.6 %fusion.15 = f32[8,1,48,1408]{3,2,0,1:T(8,128)} fusion(bf16[8,48,2048]{2,1,0:T(8,128)(2,1)S(1)} %all-to-all-done, bf16[1,2048,1408]{2,1,0:T(8,128)(2,1)} %all-gather.5.cloned.1.call-done), kind=kOutput, calls=%fused_computation.26 | convolution fusion | flops 2214592512 | bytes 9502720 | tf_op jit(solution)/shard_map/skmd,kdf->skmf/dot_general | solution.py:52
  191.0 0.3 all-gather.3.cloned.1.call-done
  191.3 8.0 %multiply_convert_fusion.1 = (bf16[8,1,48,1408]{3,2,0,1:T(8,128)(2,1)}, bf16[8,1,48,1408]{3,2,0,1:T(8,128)(2,1)S(1)}, bf16[8,1,48,1408]{3,2,0,1:T(8,128)(2,1)}) fusion(f32[8,1,48,1408]{3,2,0,1:T(8,128)} %convolution_bitcast_fusion, f32[8,1,48,1408]{3,2,0,1:T(8,128)} %fusion.15, bf16[8,48,2048]{2,1,0:T(8,128)(2,1)S(1)} %all-to-all-done, ...), kind=kOutput, calls=%fused_computation.30 | convolution fusion | flops 2223243264 | bytes 14909440 | tf_op jit(solution)/shard_map/skmd,kdf->skmf/dot_general | solution.py:51
  199.2 1.0 copy-done.6
  200.3 5.1 %fusion.2 = bf16[1,2048,1408]{2,1,0:T(8,128)(2,1)} fusion(bf16[8,48,2048]{2,1,0:T(8,128)(2,1)S(1)} %all_to_all.25, bf16[8,1,48,1408]{3,2,0,1:T(8,128)(2,1)S(1)} %get-tuple-element.17), kind=kOutput, calls=%fused_computation.13 | convolution fusion | flops 2217476096 | bytes 8421376 | tf_op jit(solution)/shard_map/skmd,skmf->kdf/dot_general | solution.py:105
  205.5 1.2 copy-done.8
  206.7 5.1 %fusion = bf16[1,2048,1408]{2,1,0:T(8,128)(2,1)} fusion(bf16[8,48,2048]{2,1,0:T(8,128)(2,1)S(1)} %all-to-all-done, bf16[8,1,48,1408]{3,2,0,1:T(8,128)(2,1)S(1)} %copy-done.8), kind=kOutput, calls=%fused_computation.11 | convolution fusion | flops 2217476096 | bytes 8421376 | tf_op jit(solution)/shard_map/skmd,skmf->kdf/dot_general | solution.py:103
  211.9 1.2 copy-done.5
  213.0 5.1 %fusion.1 = bf16[1,2048,1408]{2,1,0:T(8,128)(2,1)} fusion(bf16[8,48,2048]{2,1,0:T(8,128)(2,1)S(1)} %all-to-all-done, bf16[8,1,48,1408]{3,2,0,1:T(8,128)(2,1)S(1)} %copy-done.5), kind=kOutput, calls=%fused_computation.12 | convolution fusion | flops 2217476096 | bytes 8421376 | tf_op jit(solution)/shard_map/skmd,skmf->kdf/dot_general | solution.py:104
  218.2 4.8 %fusion.3 = f32[8,48,2048]{2,1,0:T(8,128)S(1)} fusion(bf16[1,2048,1408]{2,1,0:T(8,128)(2,1)} %all-gather.5.cloned.1.call-done, bf16[8,1,48,1408]{3,2,0,1:T(8,128)(2,1)S(1)} %copy-done.5), kind=kOutput, calls=%fused_computation.14 | convolution fusion | flops 2214592512 | bytes 9994240 | tf_op jit(solution)/shard_map/skmf,kdf->skmd/dot_general | solution.py:90
  223.1 3.8 add_convert_fusion
  226.9 4.5 all-to-all-start.4
  231.5 7.7 %convolution_convert_fusion = bf16[8,48,2048]{2,1,0:T(8,128)(2,1)} fusion(bf16[2048,1408,1]{1,0,2:T(8,128)(2,1)} %bitcast.17, bf16[8,1,48,1408]{3,2,0,1:T(8,128)(2,1)S(1)} %copy-done.7), kind=kOutput, calls=%fused_computation.28 | convolution fusion | flops 2215378944 | bytes 8421376 | tf_op jit(solution)/shard_map/skmf,kdf->skmd/dot_general | solution.py:55
  239.2 13.8 %all-to-all-done.4 = bf16[8,48,2048]{2,1,0:T(8,128)(2,1)S(1)} async-done(((bf16[8,48,2048]{2,1,0:T(8,128)(2,1)}), bf16[8,48,2048]{2,1,0:T(8,128)(2,1)S(1)}, u32[]{:S(2)}, u32[]{:S(2)}) %all-to-all-start.4) | async-done | bytes 1572896 | tf_op jit(solution)/shard_map/all_to_all | solution.py:92
  253.0 3.6 all-to-all-start.2
  256.6 2.9 convert_element_type.110
  259.7 1.5 concatenate.19
  261.2 7.0 %gather_fusion.4 = bf16[1536,2048]{1,0:T(8,128)(2,1)} fusion(bf16[385,2048]{1,0:T(8,128)(2,1)S(1)} %concatenate.19, s32[2048]{0:T(1024)S(1)} %pad_clamp_fusion), kind=kCustom, calls=%fused_computation.4 | custom fusion | bytes 12589056 | tf_op jit(solution)/shard_map/gather | solution.py:101
  268.3 11.0 %reshape.331 = bf16[256,6,2048]{2,1,0:T(8,128)(2,1)} reshape(bf16[1536,2048]{1,0:T(8,128)(2,1)} %gather_fusion.4) | data formatting | bytes 12582912 | tf_op jit(solution)/shard_map/reshape | solution.py:101
  279.2 9.8 %reduce_sum.44 = bf16[256,2048]{1,0:T(8,128)(2,1)} reduce(bf16[256,6,2048]{2,1,0:T(8,128)(2,1)} %reshape.331, bf16[]{:T(256)} %constant.31.clone.1), dimensions={1}, to_apply=%region_5.6 | reduce | flops 2621440 | bytes 7340034 | tf_op jit(solution)/shard_map/reduce_sum | solution.py:100
  289.3 7.1 %gather_fusion.1 = bf16[1536,2048]{1,0:T(8,128)(2,1)} fusion(bf16[385,2048]{1,0:T(8,128)(2,1)S(1)} %concatenate.16, s32[2048]{0:T(1024)S(1)} %pad_clamp_fusion), kind=kCustom, calls=%fused_computation.1 | custom fusion | bytes 12589056 | tf_op jit(solution)/shard_map/gather | solution.py:66
  296.3 12.0 %reshape.332 = f32[256,6,2048]{2,1,0:T(8,128)} reshape(bf16[1536,2048]{1,0:T(8,128)(2,1)} %gather_fusion.1) | data formatting | bytes 18874368 | tf_op jit(solution)/shard_map/convert_element_type | solution.py:66
  308.4 11.9 %multiply_reduce_fusion = (f32[256,6]{1,0:T(8,128)S(1)}, bf16[256,2048]{1,0:T(8,128)(2,1)}) fusion(f32[256,6,2048]{2,1,0:T(8,128)} %reshape.332, f32[256,2048]{1,0:T(8,128)S(1)} %copy-done, f32[256,6]{1,0:T(8,128)S(1)} %copy.19), kind=kLoop, calls=%fused_computation.6 | loop fusion | flops 12057088 | bytes 15740928 | tf_op jit(solution)/shard_map/reduce_sum | solution.py:70
  320.2 0.7 copy.24
  320.9 1.9 convert_element_type.119
  322.8 45.0 %reduce-scatter.4.cloned.1.call-done = bf16[1,128,1408]{2,1,0:T(8,128)(2,1)} async-done(((bf16[1,2048,1408]{2,1,0:T(8,128)(2,1)}), bf16[1,128,1408]{2,1,0:T(8,128)(2,1)}) %reduce-scatter.4.cloned.1.call-update) | async-done | bytes 360464 | tf_op jit(solution)/shard_map/reduce_scatter | solution.py:107
  367.8 1.9 convert_element_type.113
  369.7 80.7 %reduce-scatter.6.cloned.1.call-done = bf16[1,128,1408]{2,1,0:T(8,128)(2,1)} async-done(((bf16[1,2048,1408]{2,1,0:T(8,128)(2,1)}), bf16[1,128,1408]{2,1,0:T(8,128)(2,1)}) %reduce-scatter.6.cloned.1.call-update) | async-done | bytes 360464 | tf_op jit(solution)/shard_map/reduce_scatter | solution.py:110
  450.4 1.9 convert_element_type.116
  (53 shorter events, 2.0 us)
Async XLA Ops:
  7.2 15.9 %copy-start.2 = (bf16[256,2048]{1,0:T(8,128)(2,1)S(1)}, bf16[256,2048]{1,0:T(8,128)(2,1)}, u32[]{:S(2)}) copy-start(bf16[256,2048]{1,0:T(8,128)(2,1)} %param.13) | copy-start | bytes 3145732
  7.2 177.2 %all-gather.5.cloned.1.call-start = ((), (), s32[]{:S(2)}) async-start(), calls=%async_computation.9 | async-start | bytes 6127616 | tf_op jit(solution)/shard_map/all_gather | solution.py:46
  7.9 183.4 %all-gather.3.cloned.1.call-start = ((), (), s32[]{:S(2)}) async-start(), calls=%async_computation.8 | async-start | bytes 6127616 | tf_op jit(solution)/shard_map/all_gather | solution.py:45
  26.0 27.1 %copy-start.3 = (bf16[1,128,1408]{2,1,0:T(8,128)(2,1)S(1)}, bf16[1,128,1408]{2,1,0:T(8,128)(2,1)}, u32[]{:S(2)}) copy-start(bf16[1,128,1408]{2,1,0:T(8,128)(2,1)} %param.12) | copy-start | bytes 1081348
  56.2 101.5 %all-to-all-start.1 = ((bf16[16,1,128,1408]{3,2,1,0:T(8,128)(2,1)}), bf16[16,1,128,1408]{3,2,1,0:T(8,128)(2,1)}, u32[]{:S(2)}, u32[]{:S(2)}) async-start(bf16[16,1,128,1408]{3,2,1,0:T(8,128)(2,1)} %stack.2), calls=%async_computation.1 | async-start | bytes 11534336 | tf_op jit(solution)/shard_map/all_to_all | solution.py:48
  157.8 26.6 %all-to-all-start = ((bf16[8,48,2048]{2,1,0:T(8,128)(2,1)}), bf16[8,48,2048]{2,1,0:T(8,128)(2,1)S(1)}, u32[]{:S(2)}, u32[]{:S(2)}) async-start(bf16[8,48,2048]{2,1,0:T(8,128)(2,1)} %bitcast.1), calls=%async_computation | async-start | bytes 3145728 | tf_op jit(solution)/shard_map/all_to_all | solution.py:42
  162.8 158.2 %reduce-scatter.8.cloned.1.call-start = ((), (), s32[]{:S(2)}) async-start(), calls=%async_computation.12 | async-start | bytes 6127616 | tf_op jit(solution)/shard_map/reduce_scatter | solution.py:113
  199.2 1.1 copy-start.6
  205.4 1.2 copy-start.8
  205.4 162.4 %reduce-scatter.4.cloned.1.call-start = ((), (), s32[]{:S(2)}) async-start(), calls=%async_computation.10 | async-start | bytes 6127616 | tf_op jit(solution)/shard_map/reduce_scatter | solution.py:107
  211.8 1.2 copy-start.5
  211.8 238.6 %reduce-scatter.6.cloned.1.call-start = ((), (), s32[]{:S(2)}) async-start(), calls=%async_computation.11 | async-start | bytes 6127616 | tf_op jit(solution)/shard_map/reduce_scatter | solution.py:110
  218.2 4.9 %slice-start = ((s8[5767168]{0:T(1024)(128)(4,1)}), s8[1572864]{0:T(1024)(128)(4,1)S(1)}, s32[]{:S(2)}) async-start(s8[5767168]{0:T(1024)(128)(4,1)} %bitcast.108), calls=%async_computation.13 | async-start | bytes 3145728
  218.2 4.9 %slice-start.1 = ((s8[5767168]{0:T(1024)(128)(4,1)}), s8[4194304]{0:T(1024)(128)(4,1)S(1)}, s32[]{:S(2)}) async-start(s8[5767168]{0:T(1024)(128)(4,1)} %bitcast.108), calls=%async_computation.14 | async-start | bytes 8388608
  218.2 4.9 %copy-start.9 = (bf16[8,1,48,1408]{3,2,0,1:T(8,128)(2,1)S(1)}, bf16[8,1,48,1408]{3,2,0,1:T(8,128)(2,1)}, u32[]{:S(2)}) copy-start(bf16[8,1,48,1408]{3,2,0,1:T(8,128)(2,1)} %get-tuple-element.16) | copy-start | bytes 3244036
  226.9 4.5 copy-start.7
  226.9 26.1 %all-to-all-start.4 = ((bf16[8,48,2048]{2,1,0:T(8,128)(2,1)}), bf16[8,48,2048]{2,1,0:T(8,128)(2,1)S(1)}, u32[]{:S(2)}, u32[]{:S(2)}) async-start(bf16[8,48,2048]{2,1,0:T(8,128)(2,1)} %add_convert_fusion), calls=%async_computation.4 | async-start | bytes 3145728 | tf_op jit(solution)/shard_map/all_to_all | solution.py:92
  253.0 6.5 %copy-start.1 = (bf16[8,48,2048]{2,1,0:T(8,128)(2,1)}, bf16[8,48,2048]{2,1,0:T(8,128)(2,1)S(1)}, u32[]{:S(2)}) copy-start(bf16[8,48,2048]{2,1,0:T(8,128)(2,1)S(1)} %all-to-all-done.4) | copy-start | bytes 4718596
  253.0 36.1 %all-to-all-start.2 = ((bf16[8,48,2048]{2,1,0:T(8,128)(2,1)}), bf16[8,48,2048]{2,1,0:T(8,128)(2,1)S(1)}, u32[]{:S(2)}, u32[]{:S(2)}) async-start(bf16[8,48,2048]{2,1,0:T(8,128)(2,1)} %convolution_convert_fusion), calls=%async_computation.2 | async-start | bytes 3145728 | tf_op jit(solution)/shard_map/all_to_all | solution.py:58
  256.6 2.9 copy-start.4
  296.3 12.0 %copy-start = (f32[256,2048]{1,0:T(8,128)S(1)}, f32[256,2048]{1,0:T(8,128)}, u32[]{:S(2)}) copy-start(f32[256,2048]{1,0:T(8,128)} %convert_element_type.110) | copy-start | bytes 6291460
Sparse Core Ops, SparseCore 0:
  10.1 88.6 all-gather.4
  101.0 90.2 all-gather.2
  205.6 79.5 reduce-scatter.7
  288.4 79.3 reduce-scatter.3
  371.0 79.2 reduce-scatter.5
